TPU v7x, 32 devices: a whole 2x2x4 slice. The times are simulated.
32 devices in a mesh: dp: 8 (over y, x, core), seq: 4 (over z).
Axes of the slice: x: 2, y: 2, z: 4, core: 2. Of those that a mesh axis runs over, the one named last changes fastest.
Arguments:
- inputs: bfloat16 [24, 1024, 768], P('dp', 'seq'), may hold values from -6 to 6
- cotangent: bfloat16 [24, 1024, 768], P('dp', 'seq'), may hold values from -6 to 6
- lengths: int32 [24], P('dp'), may hold values from 100 to 1024, as said below
- predicted: int32 [24, 1024], P('dp', 'seq'), may hold values from 0 to 69
- norm1_gain: float32 [768], replicated, may hold values from 0.1 to 1.9
- norm1_shift: float32 [768], replicated, may hold values from -4 to 4
- w_query: bfloat16 [768, 768], replicated, may hold values from -0.3125 to 0.3125
- b_query: float32 [768], replicated, may hold values from -6 to 6
- w_key: bfloat16 [768, 768], replicated, may hold values from -0.3125 to 0.3125
- b_key: float32 [768], replicated, may hold values from -6 to 6
- w_value: bfloat16 [768, 768], replicated, may hold values from -0.21875 to 0.21875
- b_value: float32 [768], replicated, may hold values from -6 to 6
- w_out: bfloat16 [768, 768], replicated, may hold values from -2 to 2
- b_out: float32 [768], replicated, may hold values from -6 to 6
- norm2_gain: float32 [768], replicated, may hold values from 0.1 to 1.9
- norm2_shift: float32 [768], replicated, may hold values from -4 to 4
- w_up: bfloat16 [768, 3072], replicated, may hold values from -0.21875 to 0.21875
- b_up: float32 [3072], replicated, may hold values from -6 to 6
- w_down: bfloat16 [3072, 768], replicated, may hold values from -0.109375 to 0.109375
- b_down: float32 [768], replicated, may hold values from -6 to 6
Outputs:
- result: bfloat16 [24, 1024, 768], P('dp', 'seq')
- grad_inputs: bfloat16 [24, 1024, 768], P('dp', 'seq')
- grad_norm1_gain: float32 [768], replicated
- grad_norm1_shift: float32 [768], replicated
- grad_w_query: float32 [768, 768], replicated
- grad_b_query: float32 [768], replicated
- grad_w_key: float32 [768, 768], replicated
- grad_b_key: float32 [768], replicated
- grad_w_value: float32 [768, 768], replicated
- grad_b_value: float32 [768], replicated
- grad_w_out: float32 [768, 768], replicated
- grad_b_out: float32 [768], replicated
- grad_norm2_gain: float32 [768], replicated
- grad_norm2_shift: float32 [768], replicated
- grad_w_up: float32 [768, 3072], replicated
- grad_b_up: float32 [3072], replicated
- grad_w_down: float32 [3072, 768], replicated
- grad_b_down: float32 [768], replicated
- histogram: int32 [70], replicated
Inputs may be any that keep to these rules, and one draw needn't show every extreme that they name: Some sequence has 1024 real codons and some has 100; the codons from position lengths[s] on are padding.
All inputs are finite; a program needn't handle non-finite values.
Results may differ from a plain program's by a relative error of at most 0.014.
The roundings to bfloat16 on the way count: a program that leaves them out, or rounds other values in their place, can miss the bound.
Values may be sent and summed in bfloat16 or wider, within the bound.
No kernel may reach another device: no remote copies, remote signals or barrier semaphores. Data moves between devices by JAX's collectives and lax.ppermute only.
A program may use at most 192 MiB of HBM per device.

v0:
```python
import jax
import jax.numpy as jnp
from jax import lax
from jax.sharding import PartitionSpec as P

HEAD = 64
CLASSES = 70
epsilon = 1e-05


def matmul(left, right):
    return jnp.dot(left, right, preferred_element_type=jnp.float32)


def matmul_left(left, right):
    return lax.dot_general(
        left, right, (((0,), (0,)), ((), ())), preferred_element_type=jnp.float32
    )


def matmul_right(left, right):
    return lax.dot_general(
        left, right, (((1,), (1,)), ((), ())), preferred_element_type=jnp.float32
    )


def layer_norm(value, gain, shift):
    centre = value - jnp.mean(value, axis=-1, keepdims=True)
    scale = lax.rsqrt(jnp.mean(centre * centre, axis=-1, keepdims=True) + epsilon)
    return centre * scale * gain + shift


def gelu(value):
    return jax.nn.gelu(value, approximate=False)


def rotate(value, direction):
    count = value.shape[-3]
    half = value.shape[-1] // 2
    frequency = 10000.0 ** (-jnp.arange(half, dtype=jnp.float32) / half)
    angle = jnp.arange(count, dtype=jnp.float32)[:, None] * frequency[None, :]
    cosine = jnp.cos(angle)[:, None, :]
    sine = direction * jnp.sin(angle)[:, None, :]
    first = value[..., :half]
    second = value[..., half:]
    return jnp.concatenate(
        [first * cosine - second * sine, second * cosine + first * sine], axis=-1
    )


def attend_forward(query, key, value, valid, block):
    count, heads, size = query.shape
    scale = HEAD ** (-0.5)
    blocks = query.reshape(count // block, block, heads, size)

    def visit(query_block):
        scores = (
            jnp.einsum("qhd,khd->hqk", query_block, key, preferred_element_type=jnp.float32) * scale
        )
        scores = jnp.where(valid[None, None, :], scores, -1e30)
        peak = jnp.max(scores, axis=-1, keepdims=True)
        total = jnp.sum(jnp.exp(scores - peak), axis=-1, keepdims=True)
        logsum = peak + jnp.log(total)
        weights = jnp.exp(scores - logsum).astype(jnp.bfloat16)
        mixed = jnp.einsum("hqk,khd->qhd", weights, value, preferred_element_type=jnp.float32)
        return (mixed.astype(jnp.bfloat16), logsum[..., 0])

    mixed, logsum = lax.map(visit, blocks)
    return (mixed.reshape(count, heads * size), logsum)


def attend_backward(query, key, value, valid, logsum, grad_mixed, block):
    count, heads, size = query.shape
    number = count // block
    scale = HEAD ** (-0.5)
    query_blocks = query.reshape(number, block, heads, size)
    grad_blocks = grad_mixed.reshape(number, block, heads, size)

    def visit(carry, item):
        grad_key, grad_value = carry
        query_block, grad_block, logsum_block = item
        scores = (
            jnp.einsum("qhd,khd->hqk", query_block, key, preferred_element_type=jnp.float32) * scale
        )
        scores = jnp.where(valid[None, None, :], scores, -1e30)
        weights = jnp.exp(scores - logsum_block[..., None])
        weights_low = weights.astype(jnp.bfloat16)
        grad_weights = jnp.einsum(
            "qhd,khd->hqk", grad_block, value, preferred_element_type=jnp.float32
        )
        inner = jnp.sum(weights * grad_weights, axis=-1, keepdims=True)
        grad_scores = (weights * (grad_weights - inner)).astype(jnp.bfloat16)
        grad_query = (
            jnp.einsum("hqk,khd->qhd", grad_scores, key, preferred_element_type=jnp.float32) * scale
        )
        grad_key = (
            grad_key
            + jnp.einsum(
                "hqk,qhd->khd", grad_scores, query_block, preferred_element_type=jnp.float32
            )
            * scale
        )
        grad_value = grad_value + jnp.einsum(
            "hqk,qhd->khd", weights_low, grad_block, preferred_element_type=jnp.float32
        )
        return ((grad_key, grad_value), grad_query)

    start = jnp.zeros((count, heads, size), jnp.float32)
    (grad_key, grad_value), grad_query = lax.scan(
        visit, (start, start), (query_blocks, grad_blocks, logsum)
    )
    grad_query = rotate(grad_query.reshape(count, heads, size), -1.0).astype(jnp.bfloat16)
    grad_key = rotate(grad_key, -1.0).astype(jnp.bfloat16)
    grad_value = grad_value.astype(jnp.bfloat16)
    return (
        grad_query.reshape(count, heads * size),
        grad_key.reshape(count, heads * size),
        grad_value.reshape(count, heads * size),
    )


def on_device(
    inputs,
    cotangent,
    lengths,
    predicted,
    norm1_gain,
    norm1_shift,
    w_query,
    b_query,
    w_key,
    b_key,
    w_value,
    b_value,
    w_out,
    b_out,
    norm2_gain,
    norm2_shift,
    w_up,
    b_up,
    w_down,
    b_down,
):
    seqs, span, width = inputs.shape
    tokens = seqs * span
    hidden_width = w_up.shape[1]
    flat_in = inputs.reshape(tokens, width).astype(jnp.float32)
    normed_full, norm1_back = jax.vjp(layer_norm, flat_in, norm1_gain, norm1_shift)
    normed = normed_full.astype(jnp.bfloat16)
    query = (matmul(normed, w_query) + b_query).astype(jnp.bfloat16).reshape(seqs, span, width)
    key = (matmul(normed, w_key) + b_key).astype(jnp.bfloat16).reshape(seqs, span, width)
    value = (matmul(normed, w_value) + b_value).astype(jnp.bfloat16).reshape(seqs, span, width)
    head_query, head_key, head_value = (
        lax.all_to_all(query, "seq", split_axis=2, concat_axis=1, tiled=True),
        lax.all_to_all(key, "seq", split_axis=2, concat_axis=1, tiled=True),
        lax.all_to_all(value, "seq", split_axis=2, concat_axis=1, tiled=True),
    )
    count = head_query.shape[1]
    heads = head_query.shape[2] // HEAD
    shaped = (seqs, count, heads, HEAD)
    rot_query = rotate(head_query.reshape(shaped).astype(jnp.float32), 1.0).astype(jnp.bfloat16)
    rot_key = rotate(head_key.reshape(shaped).astype(jnp.float32), 1.0).astype(jnp.bfloat16)
    head_value = head_value.reshape(shaped)
    valid = jnp.arange(count)[None, :] < lengths[:, None]
    block = min(count, 512)
    mixed, logsum = lax.map(
        lambda item: attend_forward(item[0], item[1], item[2], item[3], block),
        (rot_query, rot_key, head_value, valid),
    )
    attended = lax.all_to_all(mixed, "seq", split_axis=1, concat_axis=2, tiled=True).reshape(
        tokens, width
    )
    middle = flat_in + matmul(attended, w_out) + b_out
    normed2_full, norm2_back = jax.vjp(layer_norm, middle, norm2_gain, norm2_shift)
    normed2 = normed2_full.astype(jnp.bfloat16)
    hidden_in = matmul(normed2, w_up) + b_up
    hidden = gelu(hidden_in).astype(jnp.bfloat16)
    result = (
        (middle + matmul(hidden, w_down) + b_down).astype(jnp.bfloat16).reshape(seqs, span, width)
    )
    grad_result = cotangent.reshape(tokens, width)
    grad_result_full = grad_result.astype(jnp.float32)
    grad_w_down = matmul_left(hidden, grad_result)
    grad_b_down = jnp.sum(grad_result_full, axis=0)
    unused, gelu_back = jax.vjp(gelu, hidden_in)
    grad_hidden_in = gelu_back(matmul_right(grad_result, w_down))[0].astype(jnp.bfloat16)
    grad_w_up = matmul_left(normed2, grad_hidden_in)
    grad_b_up = jnp.sum(grad_hidden_in.astype(jnp.float32), axis=0)
    grad_from_norm2, grad_norm2_gain, grad_norm2_shift = norm2_back(
        matmul_right(grad_hidden_in, w_up)
    )
    grad_middle = grad_result_full + grad_from_norm2
    grad_branch = grad_middle.astype(jnp.bfloat16)
    grad_w_out = matmul_left(attended, grad_branch)
    grad_b_out = jnp.sum(grad_middle, axis=0)
    grad_attended = matmul_right(grad_branch, w_out).astype(jnp.bfloat16).reshape(seqs, span, width)
    grad_mixed = lax.all_to_all(
        grad_attended, "seq", split_axis=2, concat_axis=1, tiled=True
    ).reshape(shaped)
    grad_query, grad_key, grad_value = lax.map(
        lambda item: attend_backward(item[0], item[1], item[2], item[3], item[4], item[5], block),
        (rot_query, rot_key, head_value, valid, logsum, grad_mixed),
    )
    back_query, back_key, back_value = (
        lax.all_to_all(grad_query, "seq", split_axis=1, concat_axis=2, tiled=True),
        lax.all_to_all(grad_key, "seq", split_axis=1, concat_axis=2, tiled=True),
        lax.all_to_all(grad_value, "seq", split_axis=1, concat_axis=2, tiled=True),
    )
    back_query = back_query.reshape(tokens, width)
    back_key = back_key.reshape(tokens, width)
    back_value = back_value.reshape(tokens, width)
    grad_w_query = matmul_left(normed, back_query)
    grad_w_key = matmul_left(normed, back_key)
    grad_w_value = matmul_left(normed, back_value)
    grad_b_query = jnp.sum(back_query.astype(jnp.float32), axis=0)
    grad_b_key = jnp.sum(back_key.astype(jnp.float32), axis=0)
    grad_b_value = jnp.sum(back_value.astype(jnp.float32), axis=0)
    grad_normed = (
        matmul_right(back_query, w_query)
        + matmul_right(back_key, w_key)
        + matmul_right(back_value, w_value)
    )
    grad_from_norm1, grad_norm1_gain, grad_norm1_shift = norm1_back(grad_normed)
    grad_inputs = (grad_middle + grad_from_norm1).astype(jnp.bfloat16).reshape(seqs, span, width)
    position = lax.axis_index("seq") * span + jnp.arange(span)
    live = position[None, :] < lengths[:, None]
    classes = jnp.arange(CLASSES)
    counts = jnp.sum(
        jnp.where(live[:, :, None] & (predicted[:, :, None] == classes), 1.0, 0.0), axis=(0, 1)
    )
    (
        grad_norm1_gain,
        grad_norm1_shift,
        grad_b_query,
        grad_b_key,
        grad_b_value,
        grad_b_out,
        grad_norm2_gain,
        grad_norm2_shift,
        grad_b_up,
        grad_b_down,
        counts,
    ) = lax.psum(
        (
            grad_norm1_gain,
            grad_norm1_shift,
            grad_b_query,
            grad_b_key,
            grad_b_value,
            grad_b_out,
            grad_norm2_gain,
            grad_norm2_shift,
            grad_b_up,
            grad_b_down,
            counts,
        ),
        ("dp", "seq"),
    )
    part_query = grad_w_query.reshape(-1)
    part_key = grad_w_key.reshape(-1)
    part_value = grad_w_value.reshape(-1)
    part_out = grad_w_out.reshape(-1)
    part_up = grad_w_up.reshape(-1)
    part_down = grad_w_down.reshape(-1)
    part_query, part_key, part_value, part_out, part_up, part_down = (
        lax.psum_scatter(part_query, ("dp", "seq"), scatter_dimension=0, tiled=True),
        lax.psum_scatter(part_key, ("dp", "seq"), scatter_dimension=0, tiled=True),
        lax.psum_scatter(part_value, ("dp", "seq"), scatter_dimension=0, tiled=True),
        lax.psum_scatter(part_out, ("dp", "seq"), scatter_dimension=0, tiled=True),
        lax.psum_scatter(part_up, ("dp", "seq"), scatter_dimension=0, tiled=True),
        lax.psum_scatter(part_down, ("dp", "seq"), scatter_dimension=0, tiled=True),
    )
    part_query, part_key, part_value, part_out, part_up, part_down = (
        lax.all_gather(part_query, ("dp", "seq"), axis=0, tiled=True),
        lax.all_gather(part_key, ("dp", "seq"), axis=0, tiled=True),
        lax.all_gather(part_value, ("dp", "seq"), axis=0, tiled=True),
        lax.all_gather(part_out, ("dp", "seq"), axis=0, tiled=True),
        lax.all_gather(part_up, ("dp", "seq"), axis=0, tiled=True),
        lax.all_gather(part_down, ("dp", "seq"), axis=0, tiled=True),
    )
    return (
        result,
        grad_inputs,
        grad_norm1_gain,
        grad_norm1_shift,
        part_query.reshape(width, width),
        grad_b_query,
        part_key.reshape(width, width),
        grad_b_key,
        part_value.reshape(width, width),
        grad_b_value,
        part_out.reshape(width, width),
        grad_b_out,
        grad_norm2_gain,
        grad_norm2_shift,
        part_up.reshape(width, hidden_width),
        grad_b_up,
        part_down.reshape(hidden_width, width),
        grad_b_down,
        counts.astype(jnp.int32),
    )


def solution(mesh):
    return jax.shard_map(
        on_device,
        mesh=mesh,
        in_specs=(
            P("dp", "seq", None),
            P("dp", "seq", None),
            P("dp"),
            P("dp", "seq"),
            P(),
            P(),
            P(),
            P(),
            P(),
            P(),
            P(),
            P(),
            P(),
            P(),
            P(),
            P(),
            P(),
            P(),
            P(),
            P(),
        ),
        out_specs=(
            P("dp", "seq", None),
            P("dp", "seq", None),
            P(),
            P(),
            P(),
            P(),
            P(),
            P(),
            P(),
            P(),
            P(),
            P(),
            P(),
            P(),
            P(),
            P(),
            P(),
            P(),
            P(),
        ),
        check_vma=False,
    )
```

profile of v0, /device:TPU:0, one launch (start us, length us, event | category | flops | bytes accessed | tf_op | source)
XLA Modules:
  0.0 1592.5 jit_solution(14903146880478550544)
XLA Ops:
  15.9 6.3 all-to-all-start.1
  22.2 3.7 add_convert_fusion.8
  26.0 3.6 copy.108
  29.5 29.6 %all-to-all-done.1 = bf16[3,256,768]{1,0,2:T(4,128)(2,1)S(1)} async-done(((bf16[3,256,768]{1,0,2:T(4,128)(2,1)}), bf16[3,256,768]{1,0,2:T(4,128)(2,1)S(1)}, u32[]{:S(2)}, u32[]{:S(2)}) %all-to-all-start.1) | async-done | bytes 1179680 | tf_op jit(solution)/shard_map/all_to_all | solution.py:155
  59.2 4.4 all-to-all-start
  70.5 29.5 %all-to-all-done = bf16[3,256,768]{1,0,2:T(4,128)(2,1)} async-done(((bf16[3,256,768]{1,0,2:T(4,128)(2,1)}), bf16[3,256,768]{1,0,2:T(4,128)(2,1)}, u32[]{:S(2)}, u32[]{:S(2)}) %all-to-all-start) | async-done | bytes 1179680 | tf_op jit(solution)/shard_map/all_to_all | solution.py:154
  100.1 4.8 all-to-all-start.2
  116.0 25.4 %all-to-all-done.2 = bf16[3,256,768]{1,0,2:T(4,128)(2,1)} async-done(((bf16[3,256,768]{1,0,2:T(4,128)(2,1)}), bf16[3,256,768]{1,0,2:T(4,128)(2,1)}, u32[]{:S(2)}, u32[]{:S(2)}) %all-to-all-start.2) | async-done | bytes 1179680 | tf_op jit(solution)/shard_map/all_to_all | solution.py:156
  153.6 43.8 %while.54 = (s32[]{:T(128)}, bf16[3,1024,192]{1,2,0:T(8,128)(2,1)}, f32[3,2,3,512]{3,2,1,0:T(4,128)}, bf16[3,1024,3,64]{1,3,2,0:T(8,128)(2,1)}, bf16[3,1024,3,64...) while((s32[]{:T(128)}, bf16[3,1024,192]{1,2,0:T(8,128)(2,1)}, ...), condition=%wide.region_7.8_spmd, body=%wide.region_2.7_spmd.sunk | while | flops 420051456 | bytes 28114308 | solution.py:166
  156.9 8.6 while.57
  171.5 8.6 while.57
  186.0 8.6 while.57
  197.4 4.3 copy.117
  201.6 51.3 %all_to_all.108 = bf16[3,1024,192]{2,0,1:T(4,128)(2,1)S(1)} all-to-all(bf16[3,1024,192]{2,0,1:T(4,128)(2,1)} %copy.117), channel_id=1, replica_groups=mesh['dp'=8,'seq'=4] {'seq'}, dimensions={1} | all-to-all | bytes 2359296 | tf_op jit(solution)/shard_map/all_to_all | solution.py:170
  262.4 7.1 fusion.73
  269.6 27.3 %convert_reduce_fusion = (f32[3072]{0:T(1024)}, bf16[768,3072]{1,0:T(8,128)(2,1)S(1)}, f32[768,3072]{1,0:T(8,128)}) fusion(f32[768,3072]{1,0:T(8,128)S(1)} %fusion.73, f32[3072]{0:T(1024)S(1)} %copy-done.58, bf16[768,768]{1,0:T(8,128)(2,1)S(1)} %bitcast.247, bf16[3072,768]{1,0:T(8,128)(2,1)S(1)} %bitcast.262), kind=kOutput, calls=%fused_computation.74 | convolution fusion | flops 3800822784 | bytes 29515776 | tf_op jit(solution)/shard_map/dot_general | solution.py:22
  296.9 4.8 multiply_reduce_fusion.1
  307.3 4.0 all-to-all-start.4
  311.3 36.0 %all-to-all-done.4 = bf16[3,256,768]{1,0,2:T(4,128)(2,1)S(1)} async-done(((bf16[3,256,768]{1,0,2:T(4,128)(2,1)}), bf16[3,256,768]{1,0,2:T(4,128)(2,1)S(1)}, u32[]{:S(2)}, u32[]{:S(2)}) %all-to-all-start.4) | async-done | bytes 1179680 | tf_op jit(solution)/shard_map/all_to_all | solution.py:197
  352.8 180.7 %while.56 = (s32[]{:T(128)}, bf16[3,1024,192]{1,2,0:T(8,128)(2,1)}, bf16[3,1024,192]{1,2,0:T(8,128)(2,1)}, bf16[3,1024,192]{1,2,0:T(8,128)(2,1)}, bf16[3,1024,3,...) while((s32[]{:T(128)}, bf16[3,1024,192]{1,2,0:T(8,128)(2,1)}, ...), condition=%wide.region_16.17_spmd, body=%wide.region_12.16_spmd.sunk | while | flops 1034713664 | bytes 145711024 | solution.py:200
  359.7 48.1 %while.58 = (s32[]{:T(128)}, f32[1024,3,64]{0,2,1:T(8,128)S(1)}, f32[1024,3,64]{0,2,1:T(8,128)}, f32[2,512,3,64]{1,0,3,2:T(2,128)}, bf16[2,512,3,64]{1,3,2,0:T(8...) while((s32[]{:T(128)}, f32[1024,3,64]{0,2,1:T(8,128)S(1)}, ...), condition=%wide.region_15.15_spmd.clone, body=%wide.region_13.14_spmd.clone.sunk | while | flops 1031305728 | bytes 117228824 | solution.py:109
  375.6 8.0 dynamic_update_slice.50
  394.5 3.8 fusion.154
  399.8 8.0 dynamic_update_slice.50
  420.0 48.1 %while.58 = (s32[]{:T(128)}, f32[1024,3,64]{0,2,1:T(8,128)S(1)}, f32[1024,3,64]{0,2,1:T(8,128)}, f32[2,512,3,64]{1,0,3,2:T(2,128)}, bf16[2,512,3,64]{1,3,2,0:T(8...) while((s32[]{:T(128)}, f32[1024,3,64]{0,2,1:T(8,128)S(1)}, ...), condition=%wide.region_15.15_spmd.clone, body=%wide.region_13.14_spmd.clone.sunk | while | flops 1031305728 | bytes 117228824 | solution.py:109
  435.8 8.0 dynamic_update_slice.50
  454.8 3.8 fusion.154
  460.0 8.0 dynamic_update_slice.50
  480.2 48.1 %while.58 = (s32[]{:T(128)}, f32[1024,3,64]{0,2,1:T(8,128)S(1)}, f32[1024,3,64]{0,2,1:T(8,128)}, f32[2,512,3,64]{1,0,3,2:T(2,128)}, bf16[2,512,3,64]{1,3,2,0:T(8...) while((s32[]{:T(128)}, f32[1024,3,64]{0,2,1:T(8,128)S(1)}, ...), condition=%wide.region_15.15_spmd.clone, body=%wide.region_13.14_spmd.clone.sunk | while | flops 1031305728 | bytes 117228824 | solution.py:109
  496.1 8.0 dynamic_update_slice.50
  515.0 3.8 fusion.154
  520.3 8.0 dynamic_update_slice.50
  533.4 4.0 copy.126
  537.5 4.6 all-to-all-start.7
  546.2 43.7 %all-to-all-done.7 = bf16[3,1024,192]{2,0,1:T(4,128)(2,1)} async-done(((bf16[3,1024,192]{2,0,1:T(4,128)(2,1)}), bf16[3,1024,192]{2,0,1:T(4,128)(2,1)}, u32[]{:S(2)}, u32[]{:S(2)}) %all-to-all-start.7) | async-done | bytes 1179680 | tf_op jit(solution)/shard_map/all_to_all | solution.py:207
  589.8 4.6 all-to-all-start.5
  594.6 10.9 convolution_bitcast_fusion
  605.5 11.0 multiply_convert_fusion.1
  619.0 23.2 %all-to-all-done.5 = bf16[3,1024,192]{2,0,1:T(4,128)(2,1)} async-done(((bf16[3,1024,192]{2,0,1:T(4,128)(2,1)}), bf16[3,1024,192]{2,0,1:T(4,128)(2,1)}, u32[]{:S(2)}, u32[]{:S(2)}) %all-to-all-start.5) | async-done | bytes 1179680 | tf_op jit(solution)/shard_map/all_to_all | solution.py:205
  642.2 4.5 all-to-all-start.6
  646.8 4.2 fusion.64
  654.4 9.7 copy.130
  664.1 8.5 fusion.84
  672.6 10.7 reshape.502
  683.4 4.9 convert_reduce_fusion.1
  688.3 4.0 reshape.490
  692.3 4.3 convert_reduce_fusion.3
  696.7 4.0 reshape.488
  700.7 4.9 convert_reduce_fusion.2
  705.6 4.4 reshape.489
  710.0 4.2 fusion.81
  717.4 4.1 fusion.82
  724.7 4.1 fusion.83
  732.2 436.6 %all-reduce.10.cloned.1.call-done = (f32[589824]{0:T(1024)}, f32[589824]{0:T(1024)}, f32[589824]{0:T(1024)}, f32[589824]{0:T(1024)}, f32[2359296]{0:T(1024)}, /*index=5*/f32[2359296]{0:T(1024)}) async-done(((f32[589824]{0:T(1024)}, f32[589824]{0:T(1024)}, f32[589824]{0:T(1024)}, f32[589824]{0:T(1024)}, f32[2359296]{0:T(1024)}, /*index=5*/f32[2359296]{0:T(1024)}), (f32[589824]{0:T(1024)}, f32[589824]{0:T(1024)}, ...) | async-done | bytes 28311568
  1180.3 9.4 add_convert_fusion.4
  1199.9 41.9 %all-reduce.6 = (f32[768]{0:T(1024)}, f32[768]{0:T(1024)}, f32[768]{0:T(1024)}, f32[768]{0:T(1024)}, f32[768]{0:T(1024)}, /*index=5*/f32[768]{0:T(1024)}, f32[76...) all-reduce(f32[768]{0:T(1024)S(1)} %get-tuple-element.328, ...), channel_id=1, replica_groups=mesh['dp'=8,'seq'=4] {'dp','seq'}, use_global_device_ids=true, to_apply=%region_20.21 | all-reduce | flops 10054 | bytes 80432 | tf_op jit(solution)/shard_map/psum | solution.py:243
  1242.3 4.2 add_convert_fusion.3
  1249.9 38.9 %all-gather.9.cloned.1.call-done = f32[589824]{0:T(1024)} async-done(((f32[18432]{0:T(1024)}), f32[589824]{0:T(1024)}) %all-gather.9.cloned.1.call-update) | async-done | bytes 2359312 | tf_op jit(solution)/shard_map/all_gather | solution.py:275
  1292.1 55.6 %all-gather.11.cloned.1.call-done = f32[589824]{0:T(1024)} async-done(((f32[18432]{0:T(1024)}), f32[589824]{0:T(1024)}) %all-gather.11.cloned.1.call-update) | async-done | bytes 2359312 | tf_op jit(solution)/shard_map/all_gather | solution.py:276
  1351.1 55.6 %all-gather.13.cloned.1.call-done = f32[589824]{0:T(1024)} async-done(((f32[18432]{0:T(1024)}), f32[589824]{0:T(1024)}) %all-gather.13.cloned.1.call-update) | async-done | bytes 2359312 | tf_op jit(solution)/shard_map/all_gather | solution.py:277
  1410.0 80.8 %all-gather.15.cloned.1.call-done = f32[2359296]{0:T(1024)} async-done(((f32[73728]{0:T(1024)}), f32[2359296]{0:T(1024)}) %all-gather.15.cloned.1.call-update) | async-done | bytes 9437200 | tf_op jit(solution)/shard_map/all_gather | solution.py:278
  1490.8 10.9 reshape.501
  1501.7 72.6 %all-gather.17.cloned.1.call-done = f32[2359296]{0:T(1024)} async-done(((f32[73728]{0:T(1024)}), f32[2359296]{0:T(1024)}) %all-gather.17.cloned.1.call-update) | async-done | bytes 9437200 | tf_op jit(solution)/shard_map/all_gather | solution.py:279
  1574.3 11.3 reshape.503
  (502 shorter events, 277.9 us)
Async XLA Ops:
  7.2 56.4 %copy-start = (bf16[768,768]{1,0:T(8,128)(2,1)S(1)}, bf16[768,768]{1,0:T(8,128)(2,1)}, u32[]{:S(2)}) copy-start(bf16[768,768]{1,0:T(8,128)(2,1)} %param.38) | copy-start | bytes 3538948
  7.2 4.1 copy-start.4
  7.2 4.1 copy-start.53
  7.2 4.1 copy-start.43
  7.2 4.6 copy-start.69
  8.9 4.8 copy-start.49
  13.7 8.5 copy-start.70
  15.9 43.3 %all-to-all-start.1 = ((bf16[3,256,768]{1,0,2:T(4,128)(2,1)}), bf16[3,256,768]{1,0,2:T(4,128)(2,1)S(1)}, u32[]{:S(2)}, u32[]{:S(2)}) async-start(bf16[3,256,768]{1,0,2:T(4,128)(2,1)} %copy.111), calls=%async_computation.1 | async-start | bytes 3145728 | tf_op jit(solution)/shard_map/all_to_all | solution.py:155
  26.0 37.6 %copy-start.71 = (f32[768]{0:T(1024)S(1)}, f32[768]{0:T(1024)}, u32[]{:S(2)}) copy-start(f32[768]{0:T(1024)} %param.39) | copy-start | bytes 9220
  59.2 40.9 %all-to-all-start = ((bf16[3,256,768]{1,0,2:T(4,128)(2,1)}), bf16[3,256,768]{1,0,2:T(4,128)(2,1)}, u32[]{:S(2)}, u32[]{:S(2)}) async-start(bf16[3,256,768]{1,0,2:T(4,128)(2,1)} %copy.108), calls=%async_computation | async-start | bytes 3145728 | tf_op jit(solution)/shard_map/all_to_all | solution.py:154
  66.9 38.0 %copy-start.65 = (s32[3]{0:T(128)S(1)}, s32[3]{0:T(128)}, u32[]{:S(2)}) copy-start(s32[3]{0:T(128)} %param.30) | copy-start | bytes 40
  100.1 41.3 %all-to-all-start.2 = ((bf16[3,256,768]{1,0,2:T(4,128)(2,1)}), bf16[3,256,768]{1,0,2:T(4,128)(2,1)}, u32[]{:S(2)}, u32[]{:S(2)}) async-start(bf16[3,256,768]{1,0,2:T(4,128)(2,1)} %copy.114), calls=%async_computation.2 | async-start | bytes 3145728 | tf_op jit(solution)/shard_map/all_to_all | solution.py:156
  143.0 4.6 copy-start.28
  143.0 4.6 copy-start.29
  197.4 55.5 %copy-start.7 = (bf16[3,1024,3,64]{1,3,2,0:T(8,128)(2,1)}, bf16[3,1024,3,64]{1,3,2,0:T(8,128)(2,1)S(1)}, u32[]{:S(2)}) copy-start(bf16[3,1024,3,64]{1,3,2,0:T(8,128)(2,1)S(1)} %get-tuple-element.910) | copy-start | bytes 3538948
  197.4 55.5 %copy-start.30 = (pred[3,1024]{1,0:T(4,128)(4,1)}, pred[3,1024]{1,0:T(4,128)(4,1)S(1)}, u32[]{:S(2)}) copy-start(pred[3,1024]{1,0:T(4,128)(4,1)S(1)} %get-tuple-element.943) | copy-start | bytes 9220
  252.9 5.8 copy-start.5
  252.9 5.8 copy-start.72
  261.6 40.2 %copy-start.8 = (f32[768,768]{1,0:T(8,128)}, f32[768,768]{1,0:T(8,128)S(1)}, u32[]{:S(2)}) copy-start(f32[768,768]{1,0:T(8,128)S(1)} %get-tuple-element.462) | copy-start | bytes 7077892
  261.7 40.1 %copy-start.35 = (f32[768]{0:T(1024)}, f32[768]{0:T(1024)S(1)}, u32[]{:S(2)}) copy-start(f32[768]{0:T(1024)S(1)} %broadcast_multiply_fusion) | copy-start | bytes 9220
  261.7 7.9 slice-start.2
  262.4 39.4 %copy-start.37 = (f32[768]{0:T(1024)}, f32[768]{0:T(1024)S(1)}, u32[]{:S(2)}) copy-start(f32[768]{0:T(1024)S(1)} %fusion.70) | copy-start | bytes 9220
  262.4 7.1 copy-start.18
  262.4 7.2 copy-start.58
  262.4 7.2 slice-start.3
  262.4 34.5 %slice-start = ((s8[4718592]{0:T(1024)(128)(4,1)}), s8[4194304]{0:T(1024)(128)(4,1)S(1)}, s32[]{:S(2)}) async-start(s8[4718592]{0:T(1024)(128)(4,1)} %bitcast.259), calls=%async_computation.15 | async-start | bytes 8388608
  269.5 27.4 %copy-start.13 = (f32[768,3072]{1,0:T(8,128)}, f32[768,3072]{1,0:T(8,128)S(1)}, u32[]{:S(2)}) copy-start(f32[768,3072]{1,0:T(8,128)S(1)} %fusion.73) | copy-start | bytes 28311556
  269.6 27.3 %slice-start.1 = ((s8[4718592]{0:T(1024)(128)(4,1)}), s8[524288]{0:T(1024)(128)(4,1)S(1)}, s32[]{:S(2)}) async-start(s8[4718592]{0:T(1024)(128)(4,1)} %bitcast.259), calls=%async_computation.16 | async-start | bytes 1048576
  296.9 4.8 copy-start.20
  307.3 40.0 %all-to-all-start.4 = ((bf16[3,256,768]{1,0,2:T(4,128)(2,1)}), bf16[3,256,768]{1,0,2:T(4,128)(2,1)S(1)}, u32[]{:S(2)}, u32[]{:S(2)}) async-start(bf16[3,256,768]{1,0,2:T(4,128)(2,1)} %copy.119), calls=%async_computation.4 | async-start | bytes 3145728 | tf_op jit(solution)/shard_map/all_to_all | solution.py:197
  366.9 3.7 copy-start.2
  390.8 3.7 copy-start.2
  394.5 3.8 copy-start.3
  427.2 3.7 copy-start.2
  451.1 3.7 copy-start.2
  454.8 3.8 copy-start.3
  487.4 3.7 copy-start.2
  515.0 3.8 copy-start.3
  537.5 4.6 copy-start.6
  537.5 4.6 copy-start.44
  537.5 4.6 copy-start.50
  537.5 4.7 copy-start.54
  537.5 4.7 copy-start.55
  537.5 6.2 copy-start.16
  537.5 52.3 %all-to-all-start.7 = ((bf16[3,1024,192]{2,0,1:T(4,128)(2,1)}), bf16[3,1024,192]{2,0,1:T(4,128)(2,1)}, u32[]{:S(2)}, u32[]{:S(2)}) async-start(bf16[3,1024,192]{2,0,1:T(4,128)(2,1)} %copy.126), calls=%async_computation.7 | async-start | bytes 4194304 | tf_op jit(solution)/shard_map/all_to_all | solution.py:207
  546.2 48.4 %copy-start.36 = (f32[768]{0:T(1024)S(1)}, f32[768]{0:T(1024)}, u32[]{:S(2)}) copy-start(f32[768]{0:T(1024)} %copy-done.35) | copy-start | bytes 9220
  546.2 48.4 %copy-start.38 = (f32[768]{0:T(1024)S(1)}, f32[768]{0:T(1024)}, u32[]{:S(2)}) copy-start(f32[768]{0:T(1024)} %copy-done.37) | copy-start | bytes 9220
  546.2 48.4 %copy-start.40 = (f32[768]{0:T(1024)S(1)}, f32[768]{0:T(1024)}, u32[]{:S(2)}) copy-start(f32[768]{0:T(1024)} %param.42) | copy-start | bytes 9220
  546.2 48.4 %copy-start.42 = (f32[768]{0:T(1024)S(1)}, f32[768]{0:T(1024)}, u32[]{:S(2)}) copy-start(f32[768]{0:T(1024)} %param.43) | copy-start | bytes 9220
  589.8 52.4 %all-to-all-start.5 = ((bf16[3,1024,192]{2,0,1:T(4,128)(2,1)}), bf16[3,1024,192]{2,0,1:T(4,128)(2,1)}, u32[]{:S(2)}, u32[]{:S(2)}) async-start(bf16[3,1024,192]{2,0,1:T(4,128)(2,1)} %copy.122), calls=%async_computation.5 | async-start | bytes 4194304 | tf_op jit(solution)/shard_map/all_to_all | solution.py:205
  594.5 10.9 copy-start.59
  605.4 11.0 copy-start.17
  619.0 27.8 %copy-start.25 = (bf16[768,768]{1,0:T(8,128)(2,1)S(1)}, bf16[768,768]{1,0:T(8,128)(2,1)}, u32[]{:S(2)}) copy-start(bf16[768,768]{1,0:T(8,128)(2,1)} %copy-done.24) | copy-start | bytes 3538948
  642.2 58.4 %all-to-all-start.6 = ((bf16[3,1024,192]{2,0,1:T(4,128)(2,1)}), bf16[3,1024,192]{2,0,1:T(4,128)(2,1)}, u32[]{:S(2)}, u32[]{:S(2)}) async-start(bf16[3,1024,192]{2,0,1:T(4,128)(2,1)} %copy.124), calls=%async_computation.6 | async-start | bytes 4194304 | tf_op jit(solution)/shard_map/all_to_all | solution.py:206
  646.7 522.1 %all-reduce.10.cloned.1.call-start = ((), (), s32[]{:S(2)}) async-start(), calls=%async_computation.14 | async-start | bytes 56623104
  654.4 9.7 copy-start.19
  732.1 447.3 %copy-start.63 = (s32[3,256]{1,0:T(4,128)S(1)}, s32[3,256]{1,0:T(4,128)}, u32[]{:S(2)}) copy-start(s32[3,256]{1,0:T(4,128)} %param.31) | copy-start | bytes 9220
  732.1 514.4 %all-gather.7.cloned.1.call-start = ((), (), s32[]{:S(2)}) async-start(), calls=%async_computation.8 | async-start | bytes 2433024 | tf_op jit(solution)/shard_map/all_gather | solution.py:274
  1170.3 118.5 %all-gather.9.cloned.1.call-start = ((), (), s32[]{:S(2)}) async-start(), calls=%async_computation.9 | async-start | bytes 2433024 | tf_op jit(solution)/shard_map/all_gather | solution.py:275
  1171.9 175.8 %all-gather.11.cloned.1.call-start = ((), (), s32[]{:S(2)}) async-start(), calls=%async_computation.10 | async-start | bytes 2433024 | tf_op jit(solution)/shard_map/all_gather | solution.py:276
  1173.5 233.1 %all-gather.13.cloned.1.call-start = ((), (), s32[]{:S(2)}) async-start(), calls=%async_computation.11 | async-start | bytes 2433024 | tf_op jit(solution)/shard_map/all_gather | solution.py:277
  1175.1 315.7 %all-gather.15.cloned.1.call-start = ((), (), s32[]{:S(2)}) async-start(), calls=%async_computation.12 | async-start | bytes 9732096 | tf_op jit(solution)/shard_map/all_gather | solution.py:278
  1176.9 397.4 %all-gather.17.cloned.1.call-start = ((), (), s32[]{:S(2)}) async-start(), calls=%async_computation.13 | async-start | bytes 9732096 | tf_op jit(solution)/shard_map/all_gather | solution.py:279
  1180.3 11.6 copy-start.26
  (70 other events, 145.4 us)
Sparse Core Ops, SparseCore 0:
  732.3 436.4 all-reduce.9
  1172.1 57.0 all-gather.6
  1232.6 56.1 all-gather.8
  1291.5 56.2 all-gather.10
  1350.4 56.2 all-gather.12
  1409.8 80.9 all-gather.14
  1493.6 80.6 all-gather.16
where the time goes:
time: 1600 us; the launch traced here: 1590 us
  waiting for transfers between devices  928 us (58%)
  local copies, waits for them, and re-layouts  257 us (16%)
  matrix products  188 us (12%)
  blocking collectives  93.2 us (6%)
  other arithmetic  77.4 us (5%)
  starting transfers between devices  33.4 us (2%)
    unnamed x8, waiting for transfers between devices  437 us
    all_gather x1, waiting for transfers between devices, on_device(): lax.all_gather(part_up, ('dp', 'seq'), axis=0, tiled=True)  80.8 us
    all_gather x1, waiting for transfers between devices, on_device(): lax.all_gather(part_down, ('dp', 'seq'), axis=0, tiled=True)  72.6 us
    all_gather x1, waiting for transfers between devices, on_device(): lax.all_gather(part_value, ('dp', 'seq'), axis=0, tiled=True)  55.6 us
    all_gather x1, waiting for transfers between devices, on_device(): lax.all_gather(part_out, ('dp', 'seq'), axis=0, tiled=True)  55.6 us
    all_to_all x1, blocking collectives, on_device(): lax.all_to_all(mixed, 'seq', split_axis=1, concat_axis=2, tiled=True)  51.3 us
    dynamic_update_slice x12, local copies, waits for them, and re-layouts, attend_backward(): lax.scan(visit, (start, start), (query_blocks, grad_blocks, logsum))  50.6 us
    all_to_all x1, waiting for transfers between devices, on_device(): lax.all_to_all(grad_value, 'seq', split_axis=1, concat_axis=2, tiled=True)  43.7 us
  transfers between devices with their start and end apart: 14, of which 12 were waited for; matrix products, arithmetic and copies ran while one was open for 10% of the time, Pallas kernels for 0%

commit v1 on v0

--- a/solution.py
+++ b/solution.py
@@ -6,6 +6,7 @@
 HEAD = 64
 CLASSES = 70
 epsilon = 1e-05
+put_rounds_over_axis = lambda piece_in: lax.psum(lax.psum(piece_in, "dp"), "seq")
 
 
 def matmul(left, right):
@@ -240,7 +241,7 @@
         grad_b_up,
         grad_b_down,
         counts,
-    ) = lax.psum(
+    ) = put_rounds_over_axis(
         (
             grad_norm1_gain,
             grad_norm1_shift,
@@ -253,8 +254,7 @@
             grad_b_up,
             grad_b_down,
             counts,
-        ),
-        ("dp", "seq"),
+        )
     )
     part_query = grad_w_query.reshape(-1)
     part_key = grad_w_key.reshape(-1)

time: 1600 us -> 1600 us (level)
    psum x1 -> x2, blocking collectives: 41.9 us -> 43.7 us  [the longest x1 24.7 us: lax.psum(piece_in, 'dp')]
where the time goes in v1:
time: 1600 us; the launch traced here: 1590 us
  waiting for transfers between devices  926 us (58%)
  local copies, waits for them, and re-layouts  257 us (16%)
  matrix products  188 us (12%)
  blocking collectives  94.9 us (6%)
  other arithmetic  77.5 us (5%)
  starting transfers between devices  33.4 us (2%)
    unnamed x8, waiting for transfers between devices  437 us
    all_gather x1, waiting for transfers between devices, on_device(): lax.all_gather(part_up, ('dp', 'seq'), axis=0, tiled=True)  80.8 us
    all_gather x1, waiting for transfers between devices, on_device(): lax.all_gather(part_down, ('dp', 'seq'), axis=0, tiled=True)  72.6 us
    all_gather x1, waiting for transfers between devices, on_device(): lax.all_gather(part_value, ('dp', 'seq'), axis=0, tiled=True)  55.6 us
    all_gather x1, waiting for transfers between devices, on_device(): lax.all_gather(part_out, ('dp', 'seq'), axis=0, tiled=True)  55.6 us
    all_to_all x1, blocking collectives, on_device(): lax.all_to_all(mixed, 'seq', split_axis=1, concat_axis=2, tiled=True)  51.3 us
    dynamic_update_slice x12, local copies, waits for them, and re-layouts, attend_backward(): lax.scan(visit, (start, start), (query_blocks, grad_blocks, logsum))  50.6 us
    all_to_all x1, waiting for transfers between devices, on_device(): lax.all_to_all(grad_value, 'seq', split_axis=1, concat_axis=2, tiled=True)  43.7 us
  transfers between devices with their start and end apart: 14, of which 12 were waited for; matrix products, arithmetic and copies ran while one was open for 10% of the time, Pallas kernels for 0%

profile of v1, /device:TPU:0, one launch (start us, length us, event | category | flops | bytes accessed | tf_op | source)
XLA Modules:
  0.0 1592.9 jit_solution(17513533751428105171)
XLA Ops:
  15.9 6.3 all-to-all-start.1
  22.2 3.7 add_convert_fusion.8
  29.5 29.6 %all-to-all-done.1 = bf16[3,256,768]{1,0,2:T(4,128)(2,1)S(1)} async-done(((bf16[3,256,768]{1,0,2:T(4,128)(2,1)}), bf16[3,256,768]{1,0,2:T(4,128)(2,1)S(1)}, u32[]{:S(2)}, u32[]{:S(2)}) %all-to-all-start.1) | async-done | bytes 1179680 | tf_op jit(solution)/shard_map/all_to_all | solution.py:156
  59.2 4.4 all-to-all-start
  70.5 29.5 %all-to-all-done = bf16[3,256,768]{1,0,2:T(4,128)(2,1)} async-done(((bf16[3,256,768]{1,0,2:T(4,128)(2,1)}), bf16[3,256,768]{1,0,2:T(4,128)(2,1)}, u32[]{:S(2)}, u32[]{:S(2)}) %all-to-all-start) | async-done | bytes 1179680 | tf_op jit(solution)/shard_map/all_to_all | solution.py:155
  100.1 4.8 all-to-all-start.2
  116.0 25.4 %all-to-all-done.2 = bf16[3,256,768]{1,0,2:T(4,128)(2,1)} async-done(((bf16[3,256,768]{1,0,2:T(4,128)(2,1)}), bf16[3,256,768]{1,0,2:T(4,128)(2,1)}, u32[]{:S(2)}, u32[]{:S(2)}) %all-to-all-start.2) | async-done | bytes 1179680 | tf_op jit(solution)/shard_map/all_to_all | solution.py:157
  153.5 43.8 %while.54 = (s32[]{:T(128)}, bf16[3,1024,192]{1,2,0:T(8,128)(2,1)}, f32[3,2,3,512]{3,2,1,0:T(4,128)}, bf16[3,1024,3,64]{1,3,2,0:T(8,128)(2,1)}, bf16[3,1024,3,64...) while((s32[]{:T(128)}, bf16[3,1024,192]{1,2,0:T(8,128)(2,1)}, ...), condition=%wide.region_7.8_spmd, body=%wide.region_2.7_spmd.sunk | while | flops 420051456 | bytes 28114308 | solution.py:167
  156.9 8.6 while.57
  171.5 8.6 while.57
  186.0 8.6 while.57
  197.4 4.3 copy.117
  201.6 51.3 %all_to_all.108 = bf16[3,1024,192]{2,0,1:T(4,128)(2,1)S(1)} all-to-all(bf16[3,1024,192]{2,0,1:T(4,128)(2,1)} %copy.117), channel_id=1, replica_groups=mesh['dp'=8,'seq'=4] {'seq'}, dimensions={1} | all-to-all | bytes 2359296 | tf_op jit(solution)/shard_map/all_to_all | solution.py:171
  262.4 7.1 fusion.73
  269.6 27.3 %convert_reduce_fusion = (f32[3072]{0:T(1024)}, bf16[768,3072]{1,0:T(8,128)(2,1)S(1)}, f32[768,3072]{1,0:T(8,128)}) fusion(f32[768,3072]{1,0:T(8,128)S(1)} %fusion.73, f32[3072]{0:T(1024)S(1)} %copy-done.58, bf16[768,768]{1,0:T(8,128)(2,1)S(1)} %bitcast.247, bf16[3072,768]{1,0:T(8,128)(2,1)S(1)} %bitcast.262), kind=kOutput, calls=%fused_computation.74 | convolution fusion | flops 3800822784 | bytes 29515776 | tf_op jit(solution)/shard_map/dot_general | solution.py:23
  296.9 4.8 multiply_reduce_fusion.1
  307.3 4.0 all-to-all-start.4
  311.3 36.0 %all-to-all-done.4 = bf16[3,256,768]{1,0,2:T(4,128)(2,1)S(1)} async-done(((bf16[3,256,768]{1,0,2:T(4,128)(2,1)}), bf16[3,256,768]{1,0,2:T(4,128)(2,1)S(1)}, u32[]{:S(2)}, u32[]{:S(2)}) %all-to-all-start.4) | async-done | bytes 1179680 | tf_op jit(solution)/shard_map/all_to_all | solution.py:198
  352.7 180.8 %while.56 = (s32[]{:T(128)}, bf16[3,1024,192]{1,2,0:T(8,128)(2,1)}, bf16[3,1024,192]{1,2,0:T(8,128)(2,1)}, bf16[3,1024,192]{1,2,0:T(8,128)(2,1)}, bf16[3,1024,3,...) while((s32[]{:T(128)}, bf16[3,1024,192]{1,2,0:T(8,128)(2,1)}, ...), condition=%wide.region_16.17_spmd, body=%wide.region_12.16_spmd.sunk | while | flops 1034713664 | bytes 145711024 | solution.py:201
  359.8 48.1 %while.58 = (s32[]{:T(128)}, f32[1024,3,64]{0,2,1:T(8,128)S(1)}, f32[1024,3,64]{0,2,1:T(8,128)}, f32[2,512,3,64]{1,0,3,2:T(2,128)}, bf16[2,512,3,64]{1,3,2,0:T(8...) while((s32[]{:T(128)}, f32[1024,3,64]{0,2,1:T(8,128)S(1)}, ...), condition=%wide.region_15.15_spmd.clone, body=%wide.region_13.14_spmd.clone.sunk | while | flops 1031305728 | bytes 117228824 | solution.py:110
  375.6 8.0 dynamic_update_slice.50
  394.6 3.8 fusion.154
  399.8 8.0 dynamic_update_slice.50
  420.0 48.1 %while.58 = (s32[]{:T(128)}, f32[1024,3,64]{0,2,1:T(8,128)S(1)}, f32[1024,3,64]{0,2,1:T(8,128)}, f32[2,512,3,64]{1,0,3,2:T(2,128)}, bf16[2,512,3,64]{1,3,2,0:T(8...) while((s32[]{:T(128)}, f32[1024,3,64]{0,2,1:T(8,128)S(1)}, ...), condition=%wide.region_15.15_spmd.clone, body=%wide.region_13.14_spmd.clone.sunk | while | flops 1031305728 | bytes 117228824 | solution.py:110
  435.9 8.0 dynamic_update_slice.50
  454.9 3.8 fusion.154
  460.1 8.0 dynamic_update_slice.50
  480.3 48.1 %while.58 = (s32[]{:T(128)}, f32[1024,3,64]{0,2,1:T(8,128)S(1)}, f32[1024,3,64]{0,2,1:T(8,128)}, f32[2,512,3,64]{1,0,3,2:T(2,128)}, bf16[2,512,3,64]{1,3,2,0:T(8...) while((s32[]{:T(128)}, f32[1024,3,64]{0,2,1:T(8,128)S(1)}, ...), condition=%wide.region_15.15_spmd.clone, body=%wide.region_13.14_spmd.clone.sunk | while | flops 1031305728 | bytes 117228824 | solution.py:110
  496.2 8.0 dynamic_update_slice.50
  515.1 3.8 fusion.154
  520.4 8.0 dynamic_update_slice.50
  533.5 4.0 copy.126
  537.6 4.6 all-to-all-start.7
  546.3 43.7 %all-to-all-done.7 = bf16[3,1024,192]{2,0,1:T(4,128)(2,1)} async-done(((bf16[3,1024,192]{2,0,1:T(4,128)(2,1)}), bf16[3,1024,192]{2,0,1:T(4,128)(2,1)}, u32[]{:S(2)}, u32[]{:S(2)}) %all-to-all-start.7) | async-done | bytes 1179680 | tf_op jit(solution)/shard_map/all_to_all | solution.py:208
  590.0 4.6 all-to-all-start.5
  594.7 10.9 convolution_bitcast_fusion
  605.6 11.0 multiply_convert_fusion.1
  619.1 23.2 %all-to-all-done.5 = bf16[3,1024,192]{2,0,1:T(4,128)(2,1)} async-done(((bf16[3,1024,192]{2,0,1:T(4,128)(2,1)}), bf16[3,1024,192]{2,0,1:T(4,128)(2,1)}, u32[]{:S(2)}, u32[]{:S(2)}) %all-to-all-start.5) | async-done | bytes 1179680 | tf_op jit(solution)/shard_map/all_to_all | solution.py:206
  642.4 4.5 all-to-all-start.6
  646.9 4.2 fusion.64
  654.5 9.7 copy.130
  664.2 8.5 fusion.84
  672.7 10.7 reshape.502
  683.5 4.9 convert_reduce_fusion.1
  688.4 4.0 reshape.490
  692.4 4.3 convert_reduce_fusion.3
  696.8 4.0 reshape.488
  700.8 4.9 convert_reduce_fusion.2
  705.7 4.4 reshape.489
  710.1 4.2 fusion.81
  717.5 4.1 fusion.82
  724.9 4.1 fusion.83
  732.3 436.6 %all-reduce.11.cloned.1.call-done = (f32[589824]{0:T(1024)}, f32[589824]{0:T(1024)}, f32[589824]{0:T(1024)}, f32[589824]{0:T(1024)}, f32[2359296]{0:T(1024)}, /*index=5*/f32[2359296]{0:T(1024)}) async-done(((f32[589824]{0:T(1024)}, f32[589824]{0:T(1024)}, f32[589824]{0:T(1024)}, f32[589824]{0:T(1024)}, f32[2359296]{0:T(1024)}, /*index=5*/f32[2359296]{0:T(1024)}), (f32[589824]{0:T(1024)}, f32[589824]{0:T(1024)}, ...) | async-done | bytes 28311568
  1180.4 9.4 add_convert_fusion.4
  1200.0 24.7 %all-reduce.7 = (f32[768]{0:T(1024)S(1)}, f32[768]{0:T(1024)S(1)}, f32[768]{0:T(1024)S(1)}, f32[768]{0:T(1024)S(1)}, f32[768]{0:T(1024)S(1)}, /*index=5*/f32[768...) all-reduce(f32[768]{0:T(1024)S(1)} %get-tuple-element.328, ...), channel_id=1, replica_groups=mesh['dp'=8,'seq'=4] {'dp'}, use_global_device_ids=true, to_apply=%region_20.21 | all-reduce | flops 10054 | bytes 80432 | tf_op jit(solution)/shard_map/psum | solution.py:9
  1224.8 18.9 %all-reduce.8 = (f32[768]{0:T(1024)}, f32[768]{0:T(1024)}, f32[768]{0:T(1024)}, f32[768]{0:T(1024)}, f32[768]{0:T(1024)}, /*index=5*/f32[768]{0:T(1024)}, f32[76...) all-reduce(f32[768]{0:T(1024)S(1)} %get-tuple-element.407, ...), channel_id=1, replica_groups=mesh['dp'=8,'seq'=4] {'seq'}, use_global_device_ids=true, to_apply=%region_21.22 | all-reduce | flops 10054 | bytes 80432 | tf_op jit(solution)/shard_map/psum | solution.py:9
  1244.2 4.2 add_convert_fusion.3
  1251.8 37.4 %all-gather.9.cloned.1.call-done = f32[589824]{0:T(1024)} async-done(((f32[18432]{0:T(1024)}), f32[589824]{0:T(1024)}) %all-gather.9.cloned.1.call-update) | async-done | bytes 2359312 | tf_op jit(solution)/shard_map/all_gather | solution.py:275
  1292.5 55.6 %all-gather.11.cloned.1.call-done = f32[589824]{0:T(1024)} async-done(((f32[18432]{0:T(1024)}), f32[589824]{0:T(1024)}) %all-gather.11.cloned.1.call-update) | async-done | bytes 2359312 | tf_op jit(solution)/shard_map/all_gather | solution.py:276
  1351.4 55.6 %all-gather.13.cloned.1.call-done = f32[589824]{0:T(1024)} async-done(((f32[18432]{0:T(1024)}), f32[589824]{0:T(1024)}) %all-gather.13.cloned.1.call-update) | async-done | bytes 2359312 | tf_op jit(solution)/shard_map/all_gather | solution.py:277
  1410.3 80.8 %all-gather.15.cloned.1.call-done = f32[2359296]{0:T(1024)} async-done(((f32[73728]{0:T(1024)}), f32[2359296]{0:T(1024)}) %all-gather.15.cloned.1.call-update) | async-done | bytes 9437200 | tf_op jit(solution)/shard_map/all_gather | solution.py:278
  1491.2 10.9 reshape.501
  1502.1 72.6 %all-gather.17.cloned.1.call-done = f32[2359296]{0:T(1024)} async-done(((f32[73728]{0:T(1024)}), f32[2359296]{0:T(1024)}) %all-gather.17.cloned.1.call-update) | async-done | bytes 9437200 | tf_op jit(solution)/shard_map/all_gather | solution.py:279
  1574.6 11.3 reshape.503
  (503 shorter events, 281.7 us)
Async XLA Ops:
  7.2 56.4 %copy-start = (bf16[768,768]{1,0:T(8,128)(2,1)S(1)}, bf16[768,768]{1,0:T(8,128)(2,1)}, u32[]{:S(2)}) copy-start(bf16[768,768]{1,0:T(8,128)(2,1)} %param.38) | copy-start | bytes 3538948
  7.2 4.1 copy-start.4
  7.2 4.1 copy-start.53
  7.2 4.1 copy-start.43
  7.2 4.6 copy-start.69
  8.9 4.8 copy-start.49
  13.7 8.5 copy-start.70
  15.9 43.3 %all-to-all-start.1 = ((bf16[3,256,768]{1,0,2:T(4,128)(2,1)}), bf16[3,256,768]{1,0,2:T(4,128)(2,1)S(1)}, u32[]{:S(2)}, u32[]{:S(2)}) async-start(bf16[3,256,768]{1,0,2:T(4,128)(2,1)} %copy.111), calls=%async_computation.1 | async-start | bytes 3145728 | tf_op jit(solution)/shard_map/all_to_all | solution.py:156
  26.0 37.6 %copy-start.71 = (f32[768]{0:T(1024)S(1)}, f32[768]{0:T(1024)}, u32[]{:S(2)}) copy-start(f32[768]{0:T(1024)} %param.39) | copy-start | bytes 9220
  59.2 40.9 %all-to-all-start = ((bf16[3,256,768]{1,0,2:T(4,128)(2,1)}), bf16[3,256,768]{1,0,2:T(4,128)(2,1)}, u32[]{:S(2)}, u32[]{:S(2)}) async-start(bf16[3,256,768]{1,0,2:T(4,128)(2,1)} %copy.108), calls=%async_computation | async-start | bytes 3145728 | tf_op jit(solution)/shard_map/all_to_all | solution.py:155
  66.9 38.0 %copy-start.65 = (s32[3]{0:T(128)S(1)}, s32[3]{0:T(128)}, u32[]{:S(2)}) copy-start(s32[3]{0:T(128)} %param.30) | copy-start | bytes 40
  100.1 41.3 %all-to-all-start.2 = ((bf16[3,256,768]{1,0,2:T(4,128)(2,1)}), bf16[3,256,768]{1,0,2:T(4,128)(2,1)}, u32[]{:S(2)}, u32[]{:S(2)}) async-start(bf16[3,256,768]{1,0,2:T(4,128)(2,1)} %copy.114), calls=%async_computation.2 | async-start | bytes 3145728 | tf_op jit(solution)/shard_map/all_to_all | solution.py:157
  143.0 4.6 copy-start.28
  143.0 4.6 copy-start.29
  197.4 55.5 %copy-start.7 = (bf16[3,1024,3,64]{1,3,2,0:T(8,128)(2,1)}, bf16[3,1024,3,64]{1,3,2,0:T(8,128)(2,1)S(1)}, u32[]{:S(2)}) copy-start(bf16[3,1024,3,64]{1,3,2,0:T(8,128)(2,1)S(1)} %get-tuple-element.921) | copy-start | bytes 3538948
  197.4 55.5 %copy-start.30 = (pred[3,1024]{1,0:T(4,128)(4,1)}, pred[3,1024]{1,0:T(4,128)(4,1)S(1)}, u32[]{:S(2)}) copy-start(pred[3,1024]{1,0:T(4,128)(4,1)S(1)} %get-tuple-element.954) | copy-start | bytes 9220
  252.9 5.8 copy-start.5
  252.9 5.8 copy-start.72
  261.6 40.2 %copy-start.8 = (f32[768,768]{1,0:T(8,128)}, f32[768,768]{1,0:T(8,128)S(1)}, u32[]{:S(2)}) copy-start(f32[768,768]{1,0:T(8,128)S(1)} %get-tuple-element.473) | copy-start | bytes 7077892
  261.7 40.1 %copy-start.35 = (f32[768]{0:T(1024)}, f32[768]{0:T(1024)S(1)}, u32[]{:S(2)}) copy-start(f32[768]{0:T(1024)S(1)} %broadcast_multiply_fusion) | copy-start | bytes 9220
  261.7 7.9 slice-start.2
  262.4 39.4 %copy-start.37 = (f32[768]{0:T(1024)}, f32[768]{0:T(1024)S(1)}, u32[]{:S(2)}) copy-start(f32[768]{0:T(1024)S(1)} %fusion.70) | copy-start | bytes 9220
  262.4 7.1 copy-start.18
  262.4 7.2 copy-start.58
  262.4 7.2 slice-start.3
  262.4 34.5 %slice-start = ((s8[4718592]{0:T(1024)(128)(4,1)}), s8[4194304]{0:T(1024)(128)(4,1)S(1)}, s32[]{:S(2)}) async-start(s8[4718592]{0:T(1024)(128)(4,1)} %bitcast.259), calls=%async_computation.15 | async-start | bytes 8388608
  269.5 27.4 %copy-start.13 = (f32[768,3072]{1,0:T(8,128)}, f32[768,3072]{1,0:T(8,128)S(1)}, u32[]{:S(2)}) copy-start(f32[768,3072]{1,0:T(8,128)S(1)} %fusion.73) | copy-start | bytes 28311556
  269.6 27.3 %slice-start.1 = ((s8[4718592]{0:T(1024)(128)(4,1)}), s8[524288]{0:T(1024)(128)(4,1)S(1)}, s32[]{:S(2)}) async-start(s8[4718592]{0:T(1024)(128)(4,1)} %bitcast.259), calls=%async_computation.16 | async-start | bytes 1048576
  296.9 4.8 copy-start.20
  307.3 40.0 %all-to-all-start.4 = ((bf16[3,256,768]{1,0,2:T(4,128)(2,1)}), bf16[3,256,768]{1,0,2:T(4,128)(2,1)S(1)}, u32[]{:S(2)}, u32[]{:S(2)}) async-start(bf16[3,256,768]{1,0,2:T(4,128)(2,1)} %copy.119), calls=%async_computation.4 | async-start | bytes 3145728 | tf_op jit(solution)/shard_map/all_to_all | solution.py:198
  366.9 3.7 copy-start.2
  390.8 3.7 copy-start.2
  394.6 3.8 copy-start.3
  427.2 3.7 copy-start.2
  451.1 3.7 copy-start.2
  454.8 3.8 copy-start.3
  511.4 3.7 copy-start.2
  515.1 3.8 copy-start.3
  537.6 4.6 copy-start.6
  537.6 4.6 copy-start.44
  537.6 4.7 copy-start.50
  537.6 4.7 copy-start.54
  537.6 4.7 copy-start.55
  537.6 6.2 copy-start.16
  537.6 52.4 %all-to-all-start.7 = ((bf16[3,1024,192]{2,0,1:T(4,128)(2,1)}), bf16[3,1024,192]{2,0,1:T(4,128)(2,1)}, u32[]{:S(2)}, u32[]{:S(2)}) async-start(bf16[3,1024,192]{2,0,1:T(4,128)(2,1)} %copy.126), calls=%async_computation.7 | async-start | bytes 4194304 | tf_op jit(solution)/shard_map/all_to_all | solution.py:208
  546.3 48.4 %copy-start.36 = (f32[768]{0:T(1024)S(1)}, f32[768]{0:T(1024)}, u32[]{:S(2)}) copy-start(f32[768]{0:T(1024)} %copy-done.35) | copy-start | bytes 9220
  546.3 48.4 %copy-start.38 = (f32[768]{0:T(1024)S(1)}, f32[768]{0:T(1024)}, u32[]{:S(2)}) copy-start(f32[768]{0:T(1024)} %copy-done.37) | copy-start | bytes 9220
  546.3 48.4 %copy-start.40 = (f32[768]{0:T(1024)S(1)}, f32[768]{0:T(1024)}, u32[]{:S(2)}) copy-start(f32[768]{0:T(1024)} %param.42) | copy-start | bytes 9220
  546.3 48.4 %copy-start.42 = (f32[768]{0:T(1024)S(1)}, f32[768]{0:T(1024)}, u32[]{:S(2)}) copy-start(f32[768]{0:T(1024)} %param.43) | copy-start | bytes 9220
  590.0 52.4 %all-to-all-start.5 = ((bf16[3,1024,192]{2,0,1:T(4,128)(2,1)}), bf16[3,1024,192]{2,0,1:T(4,128)(2,1)}, u32[]{:S(2)}, u32[]{:S(2)}) async-start(bf16[3,1024,192]{2,0,1:T(4,128)(2,1)} %copy.122), calls=%async_computation.5 | async-start | bytes 4194304 | tf_op jit(solution)/shard_map/all_to_all | solution.py:206
  594.7 10.9 copy-start.59
  605.6 11.0 copy-start.17
  619.1 27.7 %copy-start.25 = (bf16[768,768]{1,0:T(8,128)(2,1)S(1)}, bf16[768,768]{1,0:T(8,128)(2,1)}, u32[]{:S(2)}) copy-start(bf16[768,768]{1,0:T(8,128)(2,1)} %copy-done.24) | copy-start | bytes 3538948
  642.4 58.4 %all-to-all-start.6 = ((bf16[3,1024,192]{2,0,1:T(4,128)(2,1)}), bf16[3,1024,192]{2,0,1:T(4,128)(2,1)}, u32[]{:S(2)}, u32[]{:S(2)}) async-start(bf16[3,1024,192]{2,0,1:T(4,128)(2,1)} %copy.124), calls=%async_computation.6 | async-start | bytes 4194304 | tf_op jit(solution)/shard_map/all_to_all | solution.py:207
  646.8 522.1 %all-reduce.11.cloned.1.call-start = ((), (), s32[]{:S(2)}) async-start(), calls=%async_computation.14 | async-start | bytes 56623104
  654.5 9.7 copy-start.19
  732.3 447.3 %copy-start.63 = (s32[3,256]{1,0:T(4,128)S(1)}, s32[3,256]{1,0:T(4,128)}, u32[]{:S(2)}) copy-start(s32[3,256]{1,0:T(4,128)} %param.31) | copy-start | bytes 9220
  732.3 516.1 %all-gather.7.cloned.1.call-start = ((), (), s32[]{:S(2)}) async-start(), calls=%async_computation.8 | async-start | bytes 2433024 | tf_op jit(solution)/shard_map/all_gather | solution.py:274
  1170.4 118.7 %all-gather.9.cloned.1.call-start = ((), (), s32[]{:S(2)}) async-start(), calls=%async_computation.9 | async-start | bytes 2433024 | tf_op jit(solution)/shard_map/all_gather | solution.py:275
  1172.0 176.0 %all-gather.11.cloned.1.call-start = ((), (), s32[]{:S(2)}) async-start(), calls=%async_computation.10 | async-start | bytes 2433024 | tf_op jit(solution)/shard_map/all_gather | solution.py:276
  1173.6 233.3 %all-gather.13.cloned.1.call-start = ((), (), s32[]{:S(2)}) async-start(), calls=%async_computation.11 | async-start | bytes 2433024 | tf_op jit(solution)/shard_map/all_gather | solution.py:277
  1175.2 315.9 %all-gather.15.cloned.1.call-start = ((), (), s32[]{:S(2)}) async-start(), calls=%async_computation.12 | async-start | bytes 9732096 | tf_op jit(solution)/shard_map/all_gather | solution.py:278
  1177.0 397.6 %all-gather.17.cloned.1.call-start = ((), (), s32[]{:S(2)}) async-start(), calls=%async_computation.13 | async-start | bytes 9732096 | tf_op jit(solution)/shard_map/all_gather | solution.py:279
  1180.4 11.6 copy-start.26
  (70 other events, 145.4 us)
Sparse Core Ops, SparseCore 0:
  732.4 436.4 all-reduce.10
  1172.3 57.2 all-gather.6
  1233.0 56.1 all-gather.8
  1291.8 56.2 all-gather.10
  1350.7 56.2 all-gather.12
  1410.2 80.9 all-gather.14
  1494.0 80.6 all-gather.16
